TPU v7x, 32 devices: a whole 2x2x4 slice. The times are simulated.
32 devices in a mesh: feat: 8 (over z, core), col: 4 (over y, x).
Axes of the slice: x: 2, y: 2, z: 4, core: 2. Of those that a mesh axis runs over, the one named last changes fastest.
Arguments:
- self_feats: bfloat16 [4096, 128], P(('feat', 'col')), may hold values from -6 to 6
- neighbour_feats: bfloat16 [128, 16384], P('feat', 'col'), may hold values from -6 to 6
- tiles: bfloat16 [1024, 128, 128], P('col'), may hold values from 0 to 1, as said below
- tile_rows: int32 [1024], P('col'), may hold values from 0 to 31, as said below
- tile_cols: int32 [1024], P('col'), may hold values from 0 to 31
- tile_count: int32 [4], P('col'), may hold values from 1 to 256, 768 in all
- owner_order: int32 [32], replicated, may hold values from 0 to 31, as said below
- degree: int32 [4096], P(('feat', 'col')), may hold values from 64 to 192
- w_self: bfloat16 [128, 256], replicated, may hold values from -0.5 to 0.5
- w_neigh: bfloat16 [128, 256], replicated, may hold values from -0.5 to 0.5
- bias: float32 [256], replicated, may hold values from -3 to 3
- upstream: bfloat16 [4096, 256], P(('feat', 'col')), may hold values from -6 to 6
Outputs:
- hidden_out: bfloat16 [4096, 256], P(('feat', 'col'))
- neigh_grad: bfloat16 [128, 16384], P('feat', 'col')
Inputs may be any that keep to these rules, and one draw needn't show every extreme that they name: `tiles`: every entry is 0 or 1. `tile_count`: slots at or after a group's count are ignored; some group has all 256 slots live. `owner_order`: a permutation of the row blocks. `tile_rows`: in every column group, slot s has a row block whose owner position p satisfies (p) % 4 == s % 4.
All inputs are finite; a program needn't handle non-finite values.
Results may differ from a plain program's by a relative error of at most 0.0065.
Values may be sent and summed in bfloat16 or wider, within the bound.
No kernel may reach another device: no remote copies, remote signals or barrier semaphores. Data moves between devices by JAX's collectives and lax.ppermute only.
A program may use at most 64 MiB of HBM per device.

v0:
```python
import jax
import jax.numpy as jnp
from jax import lax
from jax.sharding import PartitionSpec as P


def local(
    self_feats,
    neighbour_feats,
    tiles,
    tile_rows,
    tile_cols,
    tile_count,
    owner_order,
    degree,
    w_self,
    w_neigh,
    bias,
    upstream,
):
    nfeat = lax.axis_size("feat")
    ncol = lax.axis_size("col")
    slots, tile_size, _ = tiles.shape
    slice_width = neighbour_feats.shape[0]
    col_blocks = neighbour_feats.shape[1] // tile_size
    row_blocks = self_feats.shape[0] // tile_size
    blocks_total = owner_order.shape[0]
    places = (
        jnp.zeros((blocks_total,), jnp.int32)
        .at[owner_order]
        .set(jnp.arange(blocks_total, dtype=jnp.int32))
    )
    target = places[tile_rows]
    live = (jnp.arange(slots, dtype=jnp.int32) < tile_count[0]).astype(jnp.float32)
    blocked = neighbour_feats.reshape(slice_width, col_blocks, tile_size).transpose(1, 0, 2)
    picked = blocked[tile_cols]
    products = (
        jnp.einsum("nfk,nrk->nfr", picked, tiles, preferred_element_type=jnp.float32)
        * live[:, None, None]
    )
    partial_value = (
        jnp.zeros((blocks_total, slice_width, tile_size), jnp.float32).at[target].add(products)
    )
    grid = partial_value.reshape(nfeat, ncol, row_blocks, slice_width, tile_size)
    total = lax.psum(grid, "col")
    mine = lax.dynamic_slice_in_dim(total, lax.axis_index("col"), 1, 1)
    owned = lax.all_to_all(mine, "feat", split_axis=0, concat_axis=1, tiled=True)
    summed = owned.reshape(nfeat, row_blocks, slice_width, tile_size).transpose(1, 3, 0, 2)
    summed = summed.reshape(row_blocks * tile_size, nfeat * slice_width)
    scale = lax.rsqrt(degree.astype(jnp.float32))[:, None]
    aggregate = (summed * scale).astype(jnp.bfloat16)
    pre = jnp.dot(self_feats, w_self, preferred_element_type=jnp.float32)
    pre = pre + jnp.dot(aggregate, w_neigh, preferred_element_type=jnp.float32) + bias
    gate = jax.nn.sigmoid(pre)
    hidden_out = (pre * gate).astype(jnp.bfloat16)
    slope = gate * (1.0 + pre * (1.0 - gate))
    dpre = (upstream.astype(jnp.float32) * slope).astype(jnp.bfloat16)
    dagg = lax.dot_general(
        dpre, w_neigh, (((1,), (1,)), ((), ())), preferred_element_type=jnp.float32
    )
    back = (dagg * scale).astype(jnp.bfloat16)
    arranged = back.reshape(row_blocks, tile_size, nfeat, slice_width).transpose(2, 0, 3, 1)
    arranged = arranged.reshape(nfeat, 1, row_blocks, slice_width, tile_size)
    regrouped = lax.all_to_all(arranged, "feat", split_axis=0, concat_axis=0, tiled=True)
    everything = lax.all_gather(regrouped, "col", axis=1, tiled=True)
    row_grads = everything.reshape(blocks_total, slice_width, tile_size)
    taken = row_grads[target]
    pieces = (
        jnp.einsum("nfr,nrk->nfk", taken, tiles, preferred_element_type=jnp.float32)
        * live[:, None, None]
    )
    onehot_cols = (tile_cols[:, None] == jnp.arange(col_blocks, dtype=jnp.int32)[None, :]).astype(
        jnp.float32
    )
    col_total = jnp.einsum("nc,nfk->fck", onehot_cols, pieces, precision=lax.Precision.HIGHEST)
    neigh_grad = col_total.reshape(slice_width, col_blocks * tile_size).astype(jnp.bfloat16)
    return (hidden_out, neigh_grad)


def solution(mesh):
    in_specs = (
        P(("feat", "col"), None),
        P("feat", "col"),
        P("col", None, None),
        P("col"),
        P("col"),
        P("col"),
        P(),
        P(("feat", "col")),
        P(),
        P(),
        P(),
        P(("feat", "col"), None),
    )
    out_specs = (P(("feat", "col"), None), P("feat", "col"))
    return jax.shard_map(local, mesh=mesh, in_specs=in_specs, out_specs=out_specs, check_vma=False)
```

profile of v0, /device:TPU:0, one launch (start us, length us, event | category | flops | bytes accessed | tf_op | source)
XLA Modules:
  0.0 141.6 jit_solution(16048866213782390295)
XLA Ops:
  7.2 0.0 copy-start
  7.2 0.0 all-reduce.2.cloned.1.call-start
  7.2 0.7 compare_select_fusion.3
  7.9 0.7 scatter_custom_fusion
  8.6 0.7 fusion.14
  9.3 0.7 fusion.15
  10.0 20.7 %compare_select_fusion.4 = s32[256]{0:T(256)S(1)} fusion(s32[256]{0:T(256)} %param.15, s32[]{:T(128)} %bitcast, s32[]{:T(128)} %bitcast.1, s32[]{:T(128)} %bitcast.2, s32[]{:T(128)} %bitcast.3, s32[]{:T(128)} %bitcast.4, s32[]{:T(128)} %bitcast.5, s32[]{:T(128)} %bitcast.6, s32[]{:T(128)} %bitcast.7, s32[]{:T(128)} %bitcast.8, s32[]{:T(128)} %bitcast.9, ...), kind=kLoop, calls=%fused_computation.30 | loop fusion | flops 16640 | bytes 2176 | tf_op jit(solution)/shard_map/gather | solution.py:33
  31.4 0.0 copy-done
  31.5 0.7 compare_select_fusion.1
  32.2 0.8 gather_fusion
  33.0 6.8 %convolution_multiply_fusion.1 = f32[256,16,128]{2,1,0:T(8,128)S(1)} fusion(bf16[256,16,128]{2,1,0:T(8,128)(2,1)S(1)} %gather_fusion, bf16[256,128,128]{2,1,0:T(8,128)(2,1)} %param.14, f32[256]{0:T(256)S(1)} %compare_convert_fusion), kind=kOutput, calls=%fused_computation.7 | convolution fusion | flops 134742016 | bytes 11535360 | tf_op jit(solution)/shard_map/nfk,nrk->nfr/dot_general | solution.py:38
  39.9 0.0 copy-start.2
  39.9 0.0 copy-start.3
  39.9 0.0 copy-start.8
  39.9 0.0 copy-start.5
  39.9 0.0 copy-start.7
  39.9 0.0 copy-start.6
  39.9 9.0 %scatter_fusion = f32[32,16,128]{2,1,0:T(8,128)S(1)} fusion(f32[32,16,128]{2,1,0:T(8,128)S(1)} %broadcast_in_dim.8, s32[256]{0:T(256)S(1)} %bitcast.83, f32[256,16,128]{2,1,0:T(8,128)S(1)} %convolution_multiply_fusion.1), kind=kCustom, calls=%fused_computation.3 | custom fusion | flops 524288 | bytes 6292480 | tf_op jit(solution)/shard_map/scatter-add | solution.py:42
  48.9 0.0 copy-start.1
  48.9 0.7 copy-done.1
  49.6 0.0 all-reduce.2.cloned.1.call-update
  49.6 0.0 copy-done.2
  49.6 0.0 copy-done.3
  49.6 0.1 fusion.16
  49.8 45.6 %all-reduce.2.cloned.1.call-done = f32[8,4,1,16,128]{4,3,1,0,2:T(8,128)} async-done(((f32[8,4,1,16,128]{4,3,1,0,2:T(8,128)}), f32[8,4,1,16,128]{4,3,1,0,2:T(8,128)}) %all-reduce.2.cloned.1.call-update) | async-done | bytes 262160 | tf_op jit(solution)/shard_map/psum | solution.py:45
  95.4 1.5 %dynamic-slice_bitcast_fusion = f32[8,1,1,16,128]{4,3,1,2,0:T(8,128)} fusion(f32[8,4,1,16,128]{4,3,1,0,2:T(8,128)} %all-reduce.2.cloned.1.call-done, s32[]{:T(128)S(6)} %select_n.27), kind=kLoop, calls=%fused_computation.20 | loop fusion | bytes 131076 | tf_op jit(solution)/shard_map/dynamic_slice | solution.py:46
  96.9 4.6 %all-to-all-start = ((f32[8,1,1,16,128]{4,3,1,2,0:T(8,128)}), f32[8,1,1,16,128]{4,3,1,2,0:T(8,128)S(1)}, u32[]{:S(2)}, u32[]{:S(2)}) async-start(f32[8,1,1,16,128]{4,3,1,2,0:T(8,128)} %dynamic-slice_bitcast_fusion), calls=%async_computation | async-start | bytes 131072 | tf_op jit(solution)/shard_map/all_to_all | solution.py:47
  101.5 0.0 copy-done.8
  101.5 5.9 %all-to-all-done = f32[8,1,1,16,128]{4,3,1,2,0:T(8,128)S(1)} async-done(((f32[8,1,1,16,128]{4,3,1,2,0:T(8,128)}), f32[8,1,1,16,128]{4,3,1,2,0:T(8,128)S(1)}, u32[]{:S(2)}, u32[]{:S(2)}) %all-to-all-start) | async-done | bytes 65568 | tf_op jit(solution)/shard_map/all_to_all | solution.py:47
  107.4 0.0 copy-done.5
  107.4 0.0 copy-done.7
  107.4 0.9 multiply_convert_fusion.1
  108.3 0.0 copy-done.6
  108.3 0.8 fusion.6
  109.1 3.3 %all-to-all-start.1 = ((bf16[8,1,1,16,128]{4,3,1,2,0:T(8,128)(2,1)}), bf16[8,1,1,16,128]{4,3,1,2,0:T(8,128)(2,1)S(1)}, u32[]{:S(2)}, u32[]{:S(2)}) async-start(bf16[8,1,1,16,128]{4,3,1,2,0:T(8,128)(2,1)} %bitcast.43), calls=%async_computation.1 | async-start | bytes 65536 | tf_op jit(solution)/shard_map/all_to_all | solution.py:64
  112.5 5.7 %all-to-all-done.1 = bf16[8,1,1,16,128]{4,3,1,2,0:T(8,128)(2,1)S(1)} async-done(((bf16[8,1,1,16,128]{4,3,1,2,0:T(8,128)(2,1)}), bf16[8,1,1,16,128]{4,3,1,2,0:T(8,128)(2,1)S(1)}, u32[]{:S(2)}, u32[]{:S(2)}) %all-to-all-start.1) | async-done | bytes 32800 | tf_op jit(solution)/shard_map/all_to_all | solution.py:64
  118.1 8.9 %all_gather.3 = bf16[8,4,1,16,128]{4,3,1,0,2:T(8,128)(2,1)S(1)} all-gather(bf16[8,1,1,16,128]{4,3,1,0,2:T(8,128)(2,1)S(1)} %bitcast.81), channel_id=1, replica_groups=mesh['feat'=8,'col'=4] {'col'}, dimensions={1}, use_global_device_ids=true | all-gather | bytes 163840 | tf_op jit(solution)/shard_map/all_gather | solution.py:65
  127.1 0.8 gather_fusion.1
  127.9 0.0 copy-start.4
  127.9 4.7 %convolution_multiply_fusion = f32[256,16,128]{2,1,0:T(8,128)S(1)} fusion(bf16[256,16,128]{2,1,0:T(8,128)(2,1)S(1)} %gather_fusion.1, bf16[256,128,128]{2,1,0:T(8,128)(2,1)} %param.14, f32[256]{0:T(256)S(1)} %compare_convert_fusion), kind=kOutput, calls=%fused_computation.6 | convolution fusion | flops 134742016 | bytes 11535360 | tf_op jit(solution)/shard_map/nfr,nrk->nfk/dot_general | solution.py:69
  132.6 0.0 copy-done.4
  132.6 1.4 fusion.2
  134.0 0.7 copy.30
  (9 shorter events, 0.1 us)
Async XLA Ops:
  7.2 24.3 %copy-start = (bf16[16,4096]{1,0:T(8,128)(2,1)S(1)}, bf16[16,4096]{1,0:T(8,128)(2,1)}, u32[]{:S(2)}) copy-start(bf16[16,4096]{1,0:T(8,128)(2,1)} %param.13) | copy-start | bytes 393220
  7.2 88.2 %all-reduce.2.cloned.1.call-start = ((), (), s32[]{:S(2)}) async-start(), calls=%async_computation.2 | async-start | bytes 524288 | tf_op jit(solution)/shard_map/psum | solution.py:45
  39.9 9.8 %copy-start.2 = (bf16[128,256]{1,0:T(8,128)(2,1)S(1)}, bf16[128,256]{1,0:T(8,128)(2,1)}, u32[]{:S(2)}) copy-start(bf16[128,256]{1,0:T(8,128)(2,1)} %param.20) | copy-start | bytes 196612
  39.9 9.8 %copy-start.3 = (bf16[128,128]{1,0:T(8,128)(2,1)S(1)}, bf16[128,128]{1,0:T(8,128)(2,1)}, u32[]{:S(2)}) copy-start(bf16[128,128]{1,0:T(8,128)(2,1)} %param.12) | copy-start | bytes 98308
  39.9 61.6 %copy-start.8 = (s32[128]{0:T(128)S(1)}, s32[128]{0:T(128)}, u32[]{:S(2)}) copy-start(s32[128]{0:T(128)} %param.19) | copy-start | bytes 1540
  39.9 67.5 %copy-start.5 = (bf16[128,256]{1,0:T(8,128)(2,1)S(1)}, bf16[128,256]{1,0:T(8,128)(2,1)}, u32[]{:S(2)}) copy-start(bf16[128,256]{1,0:T(8,128)(2,1)} %param.21) | copy-start | bytes 196612
  39.9 67.5 %copy-start.7 = (f32[256]{0:T(256)S(1)}, f32[256]{0:T(256)}, u32[]{:S(2)}) copy-start(f32[256]{0:T(256)} %param.22) | copy-start | bytes 3076
  39.9 68.4 %copy-start.6 = (bf16[128,256]{1,0:T(8,128)(2,1)S(1)}, bf16[128,256]{1,0:T(8,128)(2,1)}, u32[]{:S(2)}) copy-start(bf16[128,256]{1,0:T(8,128)(2,1)} %param.23) | copy-start | bytes 196612
  48.9 0.7 copy-start.1
  96.9 10.5 %all-to-all-start = ((f32[8,1,1,16,128]{4,3,1,2,0:T(8,128)}), f32[8,1,1,16,128]{4,3,1,2,0:T(8,128)S(1)}, u32[]{:S(2)}, u32[]{:S(2)}) async-start(f32[8,1,1,16,128]{4,3,1,2,0:T(8,128)} %dynamic-slice_bitcast_fusion), calls=%async_computation | async-start | bytes 131072 | tf_op jit(solution)/shard_map/all_to_all | solution.py:47
  109.1 9.0 %all-to-all-start.1 = ((bf16[8,1,1,16,128]{4,3,1,2,0:T(8,128)(2,1)}), bf16[8,1,1,16,128]{4,3,1,2,0:T(8,128)(2,1)S(1)}, u32[]{:S(2)}, u32[]{:S(2)}) async-start(bf16[8,1,1,16,128]{4,3,1,2,0:T(8,128)(2,1)} %bitcast.43), calls=%async_computation.1 | async-start | bytes 65536 | tf_op jit(solution)/shard_map/all_to_all | solution.py:64
  127.9 4.7 %copy-start.4 = (s32[256]{0:T(256)S(1)}, s32[256]{0:T(256)}, u32[]{:S(2)}) copy-start(s32[256]{0:T(256)} %param.16) | copy-start | bytes 3076
Sparse Core Ops, SparseCore 0:
  49.7 45.6 all-reduce.1
where the time goes:
time: 142 us
  waiting for transfers between devices  57.2 us (40%)
  other arithmetic  31.1 us (22%)
  between operations  14.9 us (10%)
  matrix products  14.7 us (10%)
  blocking collectives  8.92 us (6%)
  starting transfers between devices  7.98 us (6%)
  local copies, waits for them, and re-layouts  6.79 us (5%)
    psum x1, waiting for transfers between devices, local(): total = lax.psum(grid, 'col')  45.6 us
    gather x1, other arithmetic, local(): target = places[tile_rows]  20.7 us
    scatter-add x1, other arithmetic, local(): jnp.zeros((blocks_total, slice_width, tile_size), jnp.float32).at[target]  8.97 us
    all_gather x1, blocking collectives, local(): everything = lax.all_gather(regrouped, 'col', axis=1, tiled=True)  8.92 us
    dot_general x1, matrix products, local(): jnp.einsum('nfk,nrk->nfr', picked, tiles, preferred_element_type=jnp.floa...  6.77 us
    all_to_all x1, waiting for transfers between devices, local(): lax.all_to_all(mine, 'feat', split_axis=0, concat_axis=1, tiled=True)  5.9 us
    all_to_all x1, waiting for transfers between devices, local(): lax.all_to_all(arranged, 'feat', split_axis=0, concat_axis=0, tiled=True)  5.66 us
    dot_general x1, matrix products, local(): jnp.einsum('nfr,nrk->nfk', taken, tiles, preferred_element_type=jnp.float32)  4.68 us
  transfers between devices with their start and end apart: 3, of which 3 were waited for; matrix products, arithmetic and copies ran while one was open for 0% of the time, Pallas kernels for 0%

commit v1 on v0

--- a/solution.py
+++ b/solution.py
@@ -42,7 +42,7 @@
         jnp.zeros((blocks_total, slice_width, tile_size), jnp.float32).at[target].add(products)
     )
     grid = partial_value.reshape(nfeat, ncol, row_blocks, slice_width, tile_size)
-    total = lax.psum(grid, "col")
+    total = jnp.sum(lax.all_gather(grid, "col"), axis=0)
     mine = lax.dynamic_slice_in_dim(total, lax.axis_index("col"), 1, 1)
     owned = lax.all_to_all(mine, "feat", split_axis=0, concat_axis=1, tiled=True)
     summed = owned.reshape(nfeat, row_blocks, slice_width, tile_size).transpose(1, 3, 0, 2)

time: 142 us -> 126 us (0.89)
  waiting for transfers between devices: 57.2 us -> 40.9 us
    psum x1 -> x0, waiting for transfers between devices: 45.6 us -> none  [local(): total = lax.psum(grid, 'col')]
    all_gather x0 -> x1, waiting for transfers between devices: none -> 29.3 us  [local(): total = jnp.sum(lax.all_gather(grid, 'col'), axis=0)]
where the time goes in v1:
time: 126 us
  waiting for transfers between devices  40.9 us (32%)
  other arithmetic  32.4 us (26%)
  between operations  14.9 us (12%)
  matrix products  14.7 us (12%)
  blocking collectives  8.92 us (7%)
  starting transfers between devices  7.98 us (6%)
  local copies, waits for them, and re-layouts  5.93 us (5%)
    all_gather x1, waiting for transfers between devices, local(): total = jnp.sum(lax.all_gather(grid, 'col'), axis=0)  29.3 us
    gather x1, other arithmetic, local(): target = places[tile_rows]  20.7 us
    scatter-add x1, other arithmetic, local(): jnp.zeros((blocks_total, slice_width, tile_size), jnp.float32).at[target]  8.97 us
    all_gather x1, blocking collectives, local(): everything = lax.all_gather(regrouped, 'col', axis=1, tiled=True)  8.92 us
    dot_general x1, matrix products, local(): jnp.einsum('nfk,nrk->nfr', picked, tiles, preferred_element_type=jnp.floa...  6.77 us
    all_to_all x1, waiting for transfers between devices, local(): lax.all_to_all(mine, 'feat', split_axis=0, concat_axis=1, tiled=True)  5.9 us
    all_to_all x1, waiting for transfers between devices, local(): lax.all_to_all(arranged, 'feat', split_axis=0, concat_axis=0, tiled=True)  5.66 us
    dot_general x1, matrix products, local(): jnp.einsum('nfr,nrk->nfk', taken, tiles, preferred_element_type=jnp.float32)  4.68 us
  transfers between devices with their start and end apart: 3, of which 3 were waited for; matrix products, arithmetic and copies ran while one was open for 0% of the time, Pallas kernels for 0%

profile of v1, /device:TPU:0, one launch (start us, length us, event | category | flops | bytes accessed | tf_op | source)
XLA Modules:
  0.0 125.7 jit_solution(18328865845129148251)
XLA Ops:
  7.2 0.0 copy-start
  7.2 0.0 all-gather.2.cloned.1.call-start
  7.2 0.7 compare_select_fusion.3
  7.9 0.7 scatter_custom_fusion
  8.6 0.7 fusion.14
  9.3 0.7 fusion.15
  10.0 20.7 %compare_select_fusion.4 = s32[256]{0:T(256)S(1)} fusion(s32[256]{0:T(256)} %param.15, s32[]{:T(128)} %bitcast, s32[]{:T(128)} %bitcast.1, s32[]{:T(128)} %bitcast.2, s32[]{:T(128)} %bitcast.3, s32[]{:T(128)} %bitcast.4, s32[]{:T(128)} %bitcast.5, s32[]{:T(128)} %bitcast.6, s32[]{:T(128)} %bitcast.7, s32[]{:T(128)} %bitcast.8, s32[]{:T(128)} %bitcast.9, ...), kind=kLoop, calls=%fused_computation.30 | loop fusion | flops 16640 | bytes 2176 | tf_op jit(solution)/shard_map/gather | solution.py:33
  31.4 0.0 copy-done
  31.5 0.7 compare_select_fusion.1
  32.2 0.8 gather_fusion
  33.0 6.8 %convolution_multiply_fusion.1 = f32[256,16,128]{2,1,0:T(8,128)S(1)} fusion(bf16[256,16,128]{2,1,0:T(8,128)(2,1)S(1)} %gather_fusion, bf16[256,128,128]{2,1,0:T(8,128)(2,1)} %param.14, f32[256]{0:T(256)S(1)} %compare_convert_fusion), kind=kOutput, calls=%fused_computation.7 | convolution fusion | flops 134742016 | bytes 11535360 | tf_op jit(solution)/shard_map/nfk,nrk->nfr/dot_general | solution.py:38
  39.9 0.0 copy-start.2
  39.9 0.0 copy-start.3
  39.9 0.0 copy-start.8
  39.9 9.0 %scatter_fusion = f32[32,16,128]{2,1,0:T(8,128)S(1)} fusion(f32[32,16,128]{2,1,0:T(8,128)S(1)} %broadcast_in_dim.8, s32[256]{0:T(256)S(1)} %bitcast.83, f32[256,16,128]{2,1,0:T(8,128)S(1)} %convolution_multiply_fusion.1), kind=kCustom, calls=%fused_computation.3 | custom fusion | flops 524288 | bytes 6292480 | tf_op jit(solution)/shard_map/scatter-add | solution.py:42
  48.9 0.0 copy-start.1
  48.9 0.0 copy-start.5
  48.9 0.0 copy-start.7
  48.9 0.0 copy-start.6
  48.9 0.7 copy-done.1
  49.6 0.0 all-gather.2.cloned.1.call-update
  49.6 0.0 copy-done.2
  49.6 0.0 copy-done.3
  49.6 0.1 fusion.16
  49.8 29.3 %all-gather.2.cloned.1.call-done = f32[4,8,4,1,16,128]{5,4,3,2,1,0:T(8,128)} async-done(((f32[1,8,4,1,16,128]{5,4,3,2,1,0:T(8,128)}), f32[4,8,4,1,16,128]{5,4,3,2,1,0:T(8,128)}) %all-gather.2.cloned.1.call-update) | async-done | bytes 1048592 | tf_op jit(solution)/shard_map/all_gather | solution.py:45
  79.1 1.3 %reduce_sum.9 = f32[8,4,16,128]{3,2,1,0:T(8,128)S(1)} reduce(f32[4,8,4,1,16,128]{5,4,3,2,1,0:T(8,128)} %all-gather.2.cloned.1.call-done, f32[]{:T(128)} %constant.6.clone.1), dimensions={0,3}, to_apply=%region_2.0 | reduce | flops 196608 | bytes 1310724 | tf_op jit(solution)/shard_map/reduce_sum | solution.py:45
  80.4 0.6 dynamic-slice_bitcast_fusion
  81.0 4.6 %all-to-all-start = ((f32[8,1,1,16,128]{4,3,2,1,0:T(8,128)}), f32[8,1,1,16,128]{4,3,2,1,0:T(8,128)S(1)}, u32[]{:S(2)}, u32[]{:S(2)}) async-start(f32[8,1,1,16,128]{4,3,2,1,0:T(8,128)} %dynamic-slice_bitcast_fusion), calls=%async_computation | async-start | bytes 131072 | tf_op jit(solution)/shard_map/all_to_all | solution.py:47
  85.7 0.0 copy-done.8
  85.7 5.9 %all-to-all-done = f32[8,1,1,16,128]{4,3,2,1,0:T(8,128)S(1)} async-done(((f32[8,1,1,16,128]{4,3,2,1,0:T(8,128)}), f32[8,1,1,16,128]{4,3,2,1,0:T(8,128)S(1)}, u32[]{:S(2)}, u32[]{:S(2)}) %all-to-all-start) | async-done | bytes 65568 | tf_op jit(solution)/shard_map/all_to_all | solution.py:47
  91.6 0.0 copy-done.5
  91.6 0.0 copy-done.7
  91.6 0.9 multiply_convert_fusion.1
  92.5 0.0 copy-done.6
  92.5 0.8 fusion.6
  93.3 3.3 %all-to-all-start.1 = ((bf16[8,1,1,16,128]{4,3,1,2,0:T(8,128)(2,1)}), bf16[8,1,1,16,128]{4,3,1,2,0:T(8,128)(2,1)S(1)}, u32[]{:S(2)}, u32[]{:S(2)}) async-start(bf16[8,1,1,16,128]{4,3,1,2,0:T(8,128)(2,1)} %bitcast.43), calls=%async_computation.1 | async-start | bytes 65536 | tf_op jit(solution)/shard_map/all_to_all | solution.py:64
  96.6 5.7 %all-to-all-done.1 = bf16[8,1,1,16,128]{4,3,1,2,0:T(8,128)(2,1)S(1)} async-done(((bf16[8,1,1,16,128]{4,3,1,2,0:T(8,128)(2,1)}), bf16[8,1,1,16,128]{4,3,1,2,0:T(8,128)(2,1)S(1)}, u32[]{:S(2)}, u32[]{:S(2)}) %all-to-all-start.1) | async-done | bytes 32800 | tf_op jit(solution)/shard_map/all_to_all | solution.py:64
  102.3 8.9 %all_gather.7 = bf16[8,4,1,16,128]{4,3,1,0,2:T(8,128)(2,1)S(1)} all-gather(bf16[8,1,1,16,128]{4,3,1,0,2:T(8,128)(2,1)S(1)} %bitcast.81), channel_id=1, replica_groups=mesh['feat'=8,'col'=4] {'col'}, dimensions={1}, use_global_device_ids=true | all-gather | bytes 163840 | tf_op jit(solution)/shard_map/all_gather | solution.py:65
  111.2 0.8 gather_fusion.1
  112.1 0.0 copy-start.4
  112.1 4.7 %convolution_multiply_fusion = f32[256,16,128]{2,1,0:T(8,128)S(1)} fusion(bf16[256,16,128]{2,1,0:T(8,128)(2,1)S(1)} %gather_fusion.1, bf16[256,128,128]{2,1,0:T(8,128)(2,1)} %param.14, f32[256]{0:T(256)S(1)} %compare_convert_fusion), kind=kOutput, calls=%fused_computation.6 | convolution fusion | flops 134742016 | bytes 11535360 | tf_op jit(solution)/shard_map/nfr,nrk->nfk/dot_general | solution.py:69
  116.8 0.0 copy-done.4
  116.8 1.4 %fusion.2 = bf16[16,128,32]{1,2,0:T(8,128)(2,1)S(1)} fusion(f32[256,16,128]{2,1,0:T(8,128)S(1)} %convolution_multiply_fusion, s32[256]{0:T(256)S(1)} %copy-done.4), kind=kOutput, calls=%fused_computation.8 | convolution fusion | flops 201400320 | bytes 2229248 | tf_op jit(solution)/shard_map/nc,nfk->fck/dot_general | solution.py:75
  118.2 0.7 copy.32
  (9 shorter events, 0.1 us)
Async XLA Ops:
  7.2 24.3 %copy-start = (bf16[16,4096]{1,0:T(8,128)(2,1)S(1)}, bf16[16,4096]{1,0:T(8,128)(2,1)}, u32[]{:S(2)}) copy-start(bf16[16,4096]{1,0:T(8,128)(2,1)} %param.13) | copy-start | bytes 393220
  7.2 71.9 %all-gather.2.cloned.1.call-start = ((), (), s32[]{:S(2)}) async-start(), calls=%async_computation.2 | async-start | bytes 1310720 | tf_op jit(solution)/shard_map/all_gather | solution.py:45
  39.9 9.7 %copy-start.2 = (bf16[128,256]{1,0:T(8,128)(2,1)S(1)}, bf16[128,256]{1,0:T(8,128)(2,1)}, u32[]{:S(2)}) copy-start(bf16[128,256]{1,0:T(8,128)(2,1)} %param.20) | copy-start | bytes 196612
  39.9 9.7 %copy-start.3 = (bf16[128,128]{1,0:T(8,128)(2,1)S(1)}, bf16[128,128]{1,0:T(8,128)(2,1)}, u32[]{:S(2)}) copy-start(bf16[128,128]{1,0:T(8,128)(2,1)} %param.12) | copy-start | bytes 98308
  39.9 45.8 %copy-start.8 = (s32[128]{0:T(128)S(1)}, s32[128]{0:T(128)}, u32[]{:S(2)}) copy-start(s32[128]{0:T(128)} %param.19) | copy-start | bytes 1540
  48.9 0.7 copy-start.1
  48.9 42.7 %copy-start.5 = (bf16[128,256]{1,0:T(8,128)(2,1)S(1)}, bf16[128,256]{1,0:T(8,128)(2,1)}, u32[]{:S(2)}) copy-start(bf16[128,256]{1,0:T(8,128)(2,1)} %param.21) | copy-start | bytes 196612
  48.9 42.7 %copy-start.7 = (f32[256]{0:T(256)S(1)}, f32[256]{0:T(256)}, u32[]{:S(2)}) copy-start(f32[256]{0:T(256)} %param.22) | copy-start | bytes 3076
  48.9 43.6 %copy-start.6 = (bf16[128,256]{1,0:T(8,128)(2,1)S(1)}, bf16[128,256]{1,0:T(8,128)(2,1)}, u32[]{:S(2)}) copy-start(bf16[128,256]{1,0:T(8,128)(2,1)} %param.23) | copy-start | bytes 196612
  81.0 10.5 %all-to-all-start = ((f32[8,1,1,16,128]{4,3,2,1,0:T(8,128)}), f32[8,1,1,16,128]{4,3,2,1,0:T(8,128)S(1)}, u32[]{:S(2)}, u32[]{:S(2)}) async-start(f32[8,1,1,16,128]{4,3,2,1,0:T(8,128)} %dynamic-slice_bitcast_fusion), calls=%async_computation | async-start | bytes 131072 | tf_op jit(solution)/shard_map/all_to_all | solution.py:47
  93.3 9.0 %all-to-all-start.1 = ((bf16[8,1,1,16,128]{4,3,1,2,0:T(8,128)(2,1)}), bf16[8,1,1,16,128]{4,3,1,2,0:T(8,128)(2,1)S(1)}, u32[]{:S(2)}, u32[]{:S(2)}) async-start(bf16[8,1,1,16,128]{4,3,1,2,0:T(8,128)(2,1)} %bitcast.43), calls=%async_computation.1 | async-start | bytes 65536 | tf_op jit(solution)/shard_map/all_to_all | solution.py:64
  112.1 4.7 %copy-start.4 = (s32[256]{0:T(256)S(1)}, s32[256]{0:T(256)}, u32[]{:S(2)}) copy-start(s32[256]{0:T(256)} %param.16) | copy-start | bytes 3076
Sparse Core Ops, SparseCore 0:
  49.7 29.3 all-gather.1
